TPU v7x, 256 devices: a whole 4x4x8 slice. The times are simulated.
256 devices in a mesh: param: 64 (over z, x, core), ex: 4 (over y).
Axes of the slice: x: 4, y: 4, z: 8, core: 2. Of those that a mesh axis runs over, the one named last changes fastest.
Arguments:
- gradients: bfloat16 [512, 524288], P('ex', 'param'), may hold values from -60 to 60
- projection_seed: int32 [1], replicated, may hold values from 0 to 1048575
- target_features: bfloat16 [512, 4096], replicated, may hold values from -0.09375 to 0.09375
Outputs:
- scores: float32 [512, 512], P('param', 'ex')
All inputs are finite; a program needn't handle non-finite values.
Results may differ from a plain program's by a relative error of at most 0.011.
Values may be sent and summed in bfloat16 or wider, within the bound.
No kernel may reach another device: no remote copies, remote signals or barrier semaphores. Data moves between devices by JAX's collectives and lax.ppermute only.
A program may use at most 64 MiB of HBM per device.

v0:
```python
import math

import jax
import jax.numpy as jnp
from jax import lax
from jax.sharding import PartitionSpec as P

FEATS = 4096
BLOCK = 128
STEPS = 10


DAMPING = 0.001


def partner_2(array, axis, distance):
    return lax.ppermute(array, axis, [(i, i ^ 1 << distance) for i in range(lax.axis_size(axis))])


def hashed(seed_value, row_start, row_count, col_start, col_count, total_coords):
    row_index = (row_start + lax.iota(jnp.int32, row_count)).reshape(row_count, 1)
    col_index = (col_start + lax.iota(jnp.int32, col_count)).reshape(1, col_count)
    mixed = row_index * 73856093 ^ col_index * 19349663 ^ seed_value * 83492791
    mixed = mixed ^ jnp.right_shift(mixed, 13)
    mixed = mixed * 1274126177
    mixed = mixed ^ jnp.right_shift(mixed, 16)
    uniform_value = (mixed & 65535).astype(jnp.float32) * (1.0 / 65536.0)
    return ((2.0 * uniform_value - 1.0) * math.sqrt(3.0 / total_coords)).astype(jnp.bfloat16)


def newton_inverse(fisher):
    width = fisher.shape[1]
    identity = jnp.eye(width, dtype=jnp.float32)
    trace_value = jnp.einsum("bii->b", fisher)
    damped = fisher + (DAMPING * trace_value)[:, None, None] * identity
    total = jnp.einsum("bii->b", damped)
    iterate = identity[None] / total[:, None, None]
    for _ in range(STEPS):
        product = jnp.einsum("bij,bjk->bik", damped, iterate, precision=lax.Precision.HIGHEST)
        iterate = jnp.einsum(
            "bij,bjk->bik", iterate, 2.0 * identity - product, precision=lax.Precision.HIGHEST
        )
    return iterate


def to_targets(partial_scores):
    return lax.all_to_all(partial_scores, "param", split_axis=0, concat_axis=1, tiled=True)


def on_device(gradients, projection_seed, target_features):
    seed_value = projection_seed[0]
    my_index = lax.axis_index("param")
    param_count = lax.axis_size("param")
    exam_dev, coord_dev = gradients.shape
    total_coords = coord_dev * param_count
    row_start = my_index * coord_dev
    examples_total = exam_dev * lax.axis_size("ex")
    feats_owned = FEATS // param_count
    piece_width = math.gcd(feats_owned * lax.axis_size("param"), 512)

    def project_piece(col_start):
        matrix = hashed(seed_value, row_start, coord_dev, col_start, piece_width, total_coords)
        return jnp.dot(gradients, matrix, preferred_element_type=jnp.float32).T

    starts = piece_width * lax.iota(jnp.int32, feats_owned * lax.axis_size("param") // piece_width)
    pieces = lax.map(project_piece, starts)
    owned = lax.psum_scatter(
        pieces.reshape(feats_owned * lax.axis_size("param"), exam_dev),
        "param",
        scatter_dimension=0,
        tiled=True,
    ).astype(jnp.bfloat16)
    partner = partner_2(owned, "param", 0)
    is_lower = my_index % 2 == 0
    block_rows = jnp.concatenate(
        [jnp.where(is_lower, owned, partner), jnp.where(is_lower, partner, owned)], 0
    )
    block_total = block_rows.shape[0] // BLOCK
    blocks = block_rows.reshape(block_total, BLOCK, exam_dev)
    partial_fisher = jnp.einsum("bie,bje->bij", blocks, blocks, preferred_element_type=jnp.float32)
    fisher = lax.psum(partial_fisher, "ex") / examples_total
    inverse_bf = newton_inverse(fisher).astype(jnp.bfloat16)
    conditioned = jnp.einsum("bmj,bme->bje", inverse_bf, blocks, preferred_element_type=jnp.float32)
    conditioned = conditioned.astype(jnp.bfloat16).reshape(block_rows.shape[0], exam_dev)
    conditioned = lax.dynamic_slice_in_dim(conditioned, my_index % 2 * feats_owned, feats_owned, 0)
    example_rows = lax.all_to_all(conditioned, "param", split_axis=1, concat_axis=0, tiled=True)
    return to_targets(jnp.dot(target_features, example_rows, preferred_element_type=jnp.float32))


def solution(mesh):
    placed = (P("ex", "param"), P(), P())
    return jax.shard_map(
        on_device, mesh=mesh, in_specs=placed, out_specs=P("param", "ex"), check_vma=False
    )
```

profile of v0, /device:TPU:1, one launch (start us, length us, event | category | flops | bytes accessed | tf_op | source)
XLA Modules:
  0.0 352.5 jit_solution(12516402552739975225)
XLA Ops:
  7.2 89.3 %while.12 = (s32[]{:T(128)}, f32[8,512,128]{2,1,0:T(8,128)}, s32[]{:T(128)}, s32[8]{0:T(128)S(1)}, s32[]{:T(128)}, /*index=5*/bf16[128,8192]{1,0:T(8,128)(2,1)}, s32[]{:T(128)}) while((s32[]{:T(128)}, f32[8,512,128]{2,1,0:T(8,128)}, s32[]{:T(128)}, s32[8]{0:T(128)S(1)}, s32[]{:T(128)}, /*index=5*/bf16[128,8192]{1,0:T(8,128)(2,1)}, ...), condition=%wide.region_1.2_spmd, body=%wide.region_0.1_spmd.sunk | while | flops 1128285184 | bytes 2430049 | solution.py:66
  7.2 0.6 dynamic_slice.9
  7.8 0.6 add_multiply_fusion.4
  8.4 9.9 %fusion.89 = f32[8,512,128]{2,1,0:T(8,128)} fusion(f32[8,512,128]{2,1,0:T(8,128)} %get-tuple-element.145, s32[]{:T(128)} %get-tuple-element.144, bf16[128,8192]{1,0:T(8,128)(2,1)} %get-tuple-element.156, s32[]{:T(128)} %get-tuple-element.155, s32[512]{0:T(512)S(1)} %add_multiply_fusion.4, s32[8192]{0:T(1024)S(1)} %add_multiply_fusion.5), kind=kOutput, calls=%fused_computation.11.clone.1 | convolution fusion | flops 1128267776 | bytes 2395136 | tf_op jit(solution)/shard_map/while/body/eval_jaxpr/dot_general | solution.py:63
  18.4 0.6 dynamic_slice.9
  18.9 0.6 add_multiply_fusion.4
  19.6 9.9 %fusion.89 = f32[8,512,128]{2,1,0:T(8,128)} fusion(f32[8,512,128]{2,1,0:T(8,128)} %get-tuple-element.145, s32[]{:T(128)} %get-tuple-element.144, bf16[128,8192]{1,0:T(8,128)(2,1)} %get-tuple-element.156, s32[]{:T(128)} %get-tuple-element.155, s32[512]{0:T(512)S(1)} %add_multiply_fusion.4, s32[8192]{0:T(1024)S(1)} %add_multiply_fusion.5), kind=kOutput, calls=%fused_computation.11.clone.1 | convolution fusion | flops 1128267776 | bytes 2395136 | tf_op jit(solution)/shard_map/while/body/eval_jaxpr/dot_general | solution.py:63
  29.5 0.6 dynamic_slice.9
  30.1 0.6 add_multiply_fusion.4
  30.7 9.9 %fusion.89 = f32[8,512,128]{2,1,0:T(8,128)} fusion(f32[8,512,128]{2,1,0:T(8,128)} %get-tuple-element.145, s32[]{:T(128)} %get-tuple-element.144, bf16[128,8192]{1,0:T(8,128)(2,1)} %get-tuple-element.156, s32[]{:T(128)} %get-tuple-element.155, s32[512]{0:T(512)S(1)} %add_multiply_fusion.4, s32[8192]{0:T(1024)S(1)} %add_multiply_fusion.5), kind=kOutput, calls=%fused_computation.11.clone.1 | convolution fusion | flops 1128267776 | bytes 2395136 | tf_op jit(solution)/shard_map/while/body/eval_jaxpr/dot_general | solution.py:63
  40.7 0.6 dynamic_slice.9
  41.2 0.6 add_multiply_fusion.4
  41.9 9.9 %fusion.89 = f32[8,512,128]{2,1,0:T(8,128)} fusion(f32[8,512,128]{2,1,0:T(8,128)} %get-tuple-element.145, s32[]{:T(128)} %get-tuple-element.144, bf16[128,8192]{1,0:T(8,128)(2,1)} %get-tuple-element.156, s32[]{:T(128)} %get-tuple-element.155, s32[512]{0:T(512)S(1)} %add_multiply_fusion.4, s32[8192]{0:T(1024)S(1)} %add_multiply_fusion.5), kind=kOutput, calls=%fused_computation.11.clone.1 | convolution fusion | flops 1128267776 | bytes 2395136 | tf_op jit(solution)/shard_map/while/body/eval_jaxpr/dot_general | solution.py:63
  51.8 0.6 dynamic_slice.9
  52.4 0.6 add_multiply_fusion.4
  53.0 9.9 %fusion.89 = f32[8,512,128]{2,1,0:T(8,128)} fusion(f32[8,512,128]{2,1,0:T(8,128)} %get-tuple-element.145, s32[]{:T(128)} %get-tuple-element.144, bf16[128,8192]{1,0:T(8,128)(2,1)} %get-tuple-element.156, s32[]{:T(128)} %get-tuple-element.155, s32[512]{0:T(512)S(1)} %add_multiply_fusion.4, s32[8192]{0:T(1024)S(1)} %add_multiply_fusion.5), kind=kOutput, calls=%fused_computation.11.clone.1 | convolution fusion | flops 1128267776 | bytes 2395136 | tf_op jit(solution)/shard_map/while/body/eval_jaxpr/dot_general | solution.py:63
  63.0 0.6 dynamic_slice.9
  63.6 0.6 add_multiply_fusion.4
  64.2 9.9 %fusion.89 = f32[8,512,128]{2,1,0:T(8,128)} fusion(f32[8,512,128]{2,1,0:T(8,128)} %get-tuple-element.145, s32[]{:T(128)} %get-tuple-element.144, bf16[128,8192]{1,0:T(8,128)(2,1)} %get-tuple-element.156, s32[]{:T(128)} %get-tuple-element.155, s32[512]{0:T(512)S(1)} %add_multiply_fusion.4, s32[8192]{0:T(1024)S(1)} %add_multiply_fusion.5), kind=kOutput, calls=%fused_computation.11.clone.1 | convolution fusion | flops 1128267776 | bytes 2395136 | tf_op jit(solution)/shard_map/while/body/eval_jaxpr/dot_general | solution.py:63
  74.2 0.6 dynamic_slice.9
  74.7 0.6 add_multiply_fusion.4
  75.4 9.9 %fusion.89 = f32[8,512,128]{2,1,0:T(8,128)} fusion(f32[8,512,128]{2,1,0:T(8,128)} %get-tuple-element.145, s32[]{:T(128)} %get-tuple-element.144, bf16[128,8192]{1,0:T(8,128)(2,1)} %get-tuple-element.156, s32[]{:T(128)} %get-tuple-element.155, s32[512]{0:T(512)S(1)} %add_multiply_fusion.4, s32[8192]{0:T(1024)S(1)} %add_multiply_fusion.5), kind=kOutput, calls=%fused_computation.11.clone.1 | convolution fusion | flops 1128267776 | bytes 2395136 | tf_op jit(solution)/shard_map/while/body/eval_jaxpr/dot_general | solution.py:63
  85.3 0.6 dynamic_slice.9
  85.9 0.6 add_multiply_fusion.4
  86.5 9.9 %fusion.89 = f32[8,512,128]{2,1,0:T(8,128)} fusion(f32[8,512,128]{2,1,0:T(8,128)} %get-tuple-element.145, s32[]{:T(128)} %get-tuple-element.144, bf16[128,8192]{1,0:T(8,128)(2,1)} %get-tuple-element.156, s32[]{:T(128)} %get-tuple-element.155, s32[512]{0:T(512)S(1)} %add_multiply_fusion.4, s32[8192]{0:T(1024)S(1)} %add_multiply_fusion.5), kind=kOutput, calls=%fused_computation.11.clone.1 | convolution fusion | flops 1128267776 | bytes 2395136 | tf_op jit(solution)/shard_map/while/body/eval_jaxpr/dot_general | solution.py:63
  96.5 0.0 all-reduce.2.cloned.1.call-start
  96.5 140.2 %reduce-scatter.2.cloned.1.call-done = f32[64,128]{1,0:T(8,128)} async-done(((f32[4096,128]{1,0:T(8,128)}), f32[64,128]{1,0:T(8,128)}) %reduce-scatter.2.cloned.1.call-update) | async-done | bytes 32784 | tf_op jit(solution)/shard_map/reduce_scatter | solution.py:67
  236.7 0.8 convert_element_type.28
  237.5 5.9 %collective-permute-start = (bf16[64,128]{1,0:T(8,128)(2,1)S(1)}, bf16[64,128]{1,0:T(8,128)(2,1)S(1)}, u32[]{:S(2)}, u32[]{:S(2)}) collective-permute-start(bf16[64,128]{1,0:T(8,128)(2,1)S(1)} %convert_element_type.28), channel_id=1, source_target_pairs={{0,4},{4,0},{8,12},{12,8},{16,20},{20,16},{24,28},{28,24},{32,36},... | collective-permute-start | bytes 49160 | tf_op jit(solution)/shard_map/ppermute | solution.py:17
  243.4 0.8 collective-permute-done
  244.2 0.8 broadcast_select_fusion.1
  245.0 0.8 convolution_bitcast_fusion
  245.8 42.4 %all-reduce.2.cloned.1.call-done = f32[1,128,128]{2,1,0:T(8,128)} async-done(((f32[1,128,128]{2,1,0:T(8,128)}), f32[1,128,128]{2,1,0:T(8,128)}) %all-reduce.2.cloned.1.call-update) | async-done | bytes 65552 | tf_op jit(solution)/shard_map/psum | solution.py:81
  288.2 1.5 select_reduce_fusion.1
  290.3 1.5 select_reduce_fusion
  292.5 1.0 convolution_subtract_fusion.9
  293.5 0.2 fusion.22
  293.7 1.0 convolution_subtract_fusion.8
  294.8 0.2 fusion.44
  295.0 1.0 convolution_subtract_fusion.7
  296.0 0.2 fusion.45
  296.3 1.0 convolution_subtract_fusion.6
  297.3 0.2 fusion.46
  297.5 1.0 convolution_subtract_fusion.5
  298.6 0.2 fusion.47
  298.8 1.0 convolution_subtract_fusion.4
  299.8 0.2 fusion.48
  300.1 1.0 convolution_subtract_fusion.3
  301.1 0.2 fusion.49
  301.3 1.0 convolution_subtract_fusion.2
  302.4 0.2 fusion.50
  302.6 1.0 convolution_subtract_fusion.1
  303.6 0.2 fusion.51
  303.9 1.0 convolution_subtract_fusion
  304.9 0.2 convolution_convert_fusion
  305.1 0.2 fusion.39
  305.3 0.1 copy.9
  305.4 21.9 %all_to_all.38 = bf16[64,64,2]{0,2,1:T(2,128)(2,1)S(1)} all-to-all(bf16[64,64,2]{0,2,1:T(2,128)(2,1)S(1)} %bitcast.81), channel_id=1, replica_groups=mesh['param'=64,'ex'=4] {'param'}, dimensions={1} | all-to-all | bytes 32768 | tf_op jit(solution)/shard_map/all_to_all | solution.py:86
  327.3 0.1 all_to_all.31
  327.4 3.4 convolution_bitcast_fusion.1
  330.8 0.1 all_to_all.32
  330.9 0.1 copy.11
  331.0 14.0 %all_to_all.39 = f32[64,8,2]{1,2,0:T(2,128)S(1)} all-to-all(f32[64,8,2]{1,2,0:T(2,128)S(1)} %copy.11), channel_id=1, replica_groups=mesh['param'=64,'ex'=4] {'param'}, dimensions={0} | all-to-all | bytes 8192 | tf_op jit(solution)/shard_map/all_to_all | solution.py:47
  345.0 0.7 copy.12
  (15 shorter events, 0.1 us)
Async XLA Ops:
  6.5 230.2 %reduce-scatter.2.cloned.1.call-start = ((), (), s32[]{:S(2)}) async-start(), calls=%async_computation.3 | async-start | bytes 2129920 | tf_op jit(solution)/shard_map/reduce_scatter | solution.py:67
  96.5 191.7 %all-reduce.2.cloned.1.call-start = ((), (), s32[]{:S(2)}) async-start(), calls=%async_computation.4 | async-start | bytes 131072 | tf_op jit(solution)/shard_map/psum | solution.py:81
  237.5 6.7 %collective-permute-start = (bf16[64,128]{1,0:T(8,128)(2,1)S(1)}, bf16[64,128]{1,0:T(8,128)(2,1)S(1)}, u32[]{:S(2)}, u32[]{:S(2)}) collective-permute-start(bf16[64,128]{1,0:T(8,128)(2,1)S(1)} %convert_element_type.28), channel_id=1, source_target_pairs={{0,4},{4,0},{8,12},{12,8},{16,20},{20,16},{24,28},{28,24},{32,36},... | collective-permute-start | bytes 49160 | tf_op jit(solution)/shard_map/ppermute | solution.py:17
Sparse Core Ops, SparseCore 0:
  96.6 140.0 reduce-scatter.1
  245.9 42.2 all-reduce.1
where the time goes:
time: 354 us; the launch traced here: 352 us
  waiting for transfers between devices  183 us (52%)
  matrix products  96.2 us (27%)
  blocking collectives  35.9 us (10%)
  between operations  15.6 us (4%)
  other arithmetic  9.49 us (3%)
  starting transfers between devices  5.94 us (2%)
  local copies, waits for them, and re-layouts  5.78 us (2%)
    reduce_scatter x1, waiting for transfers between devices, on_device(): lax.psum_scatter(pieces.reshape(feats_owned * lax.axis_size('param'), exa...  140 us
    dot_general x8, matrix products, project_piece(): return jnp.dot(gradients, matrix, preferred_element_type=jnp.float32).T  79.4 us
    psum x1, waiting for transfers between devices, on_device(): fisher = lax.psum(partial_fisher, 'ex') / examples_total  42.4 us
    all_to_all x1, blocking collectives, on_device(): lax.all_to_all(conditioned, 'param', split_axis=1, concat_axis=0, tiled=T...  21.9 us
    all_to_all x1, blocking collectives, to_targets(): lax.all_to_all(partial_scores, 'param', split_axis=0, concat_axis=1, tile...  14 us
    dot_general x10, matrix products, newton_inverse(): jnp.einsum('bij,bjk->bik', damped, iterate, precision=lax.Precision.HIGHEST)  10.5 us
  transfers between devices with their start and end apart: 3, of which 3 were waited for; matrix products, arithmetic and copies ran while one was open for 0% of the time, Pallas kernels for 0%

commit v1 on v0

v1 whole, which is shorter than its diff:
```python
import functools
import math

import jax
import jax.numpy as jnp
from jax import lax
from jax.experimental import pallas as pl
from jax.experimental.pallas import tpu as pltpu
from jax.sharding import Mesh
from jax.sharding import PartitionSpec as P

FEATS = 4096
BLOCK = 128
STEPS = 10
DAMPING = 0.001

ROW_MUL = 73856093
COL_MUL = 19349663
SEED_MUL = 83492791
MIX_MUL = 1274126177
TOP_BIT = -(2**31)
HIGH_HALF = -65536

FEAT_TILE = 256
COORD_TILE = 2048
INIT_TILE = 256


def fold13(value):
    return value ^ jnp.right_shift(value, 13)


def project_kernel(seed_ref, grad_ref, own_ref, send_ref, rows_ref, *, scale):
    step = pl.program_id(0)
    coord_dev = grad_ref.shape[1]
    half = own_ref.shape[1]
    core = lax.axis_index("c")
    chip = lax.axis_index("z") * lax.axis_size("x") + lax.axis_index("x")
    row_start = (chip * lax.axis_size("c") + core) * coord_dev

    @pl.when(step == 0)
    def _():
        def fill(i, carry):
            start = pl.multiple_of(i * INIT_TILE, INIT_TILE)
            rows = lax.broadcasted_iota(jnp.int32, (INIT_TILE, 128), 0) + (row_start + start)
            rows_ref[pl.ds(start, INIT_TILE), :] = fold13(rows * ROW_MUL)
            return carry

        lax.fori_loop(0, coord_dev // INIT_TILE, fill, 0)

    columns = []
    for lane_tile in range(FEAT_TILE // 128):
        first = step * FEAT_TILE + lane_tile * 128
        col = first + lax.broadcasted_iota(jnp.int32, (1, 128), 1)
        columns.append(fold13(col * COL_MUL ^ seed_ref[0] * SEED_MUL) ^ TOP_BIT)

    def add_tile(i, total):
        start = pl.multiple_of(i * COORD_TILE, COORD_TILE)
        rows = rows_ref[pl.ds(start, COORD_TILE), :]
        tiles = []
        for column in columns:
            mixed = (rows ^ column) * MIX_MUL
            centred = (mixed ^ jnp.left_shift(mixed, 16)) & HIGH_HALF
            value = centred.astype(jnp.float32) * (scale * 2.0**-31)
            tiles.append(value.astype(jnp.bfloat16))
        return total + jnp.dot(
            grad_ref[:, pl.ds(start, COORD_TILE)],
            jnp.concatenate(tiles, 1),
            preferred_element_type=jnp.float32,
        )

    total = lax.fori_loop(
        0, coord_dev // COORD_TILE, add_tile, jnp.zeros((2 * half, FEAT_TILE), jnp.float32)
    )
    for j in range(FEAT_TILE // BLOCK):
        part = total[:, j * BLOCK : (j + 1) * BLOCK]

        @pl.when(core == 0)
        def _():
            own_ref[j] = part[:half]
            send_ref[j] = part[half:]

        @pl.when(core == 1)
        def _():
            own_ref[j] = part[half:]
            send_ref[j] = part[:half]


def project(gradients, projection_seed):
    exam_dev, coord_dev = gradients.shape
    total_coords = coord_dev * lax.axis_size(("z", "x", "c"))
    blocks = FEATS // BLOCK
    out = jax.ShapeDtypeStruct((blocks, exam_dev // 2, BLOCK), jnp.float32)
    block = pl.BlockSpec((FEAT_TILE // BLOCK, exam_dev // 2, BLOCK), lambda i, s: (i, 0, 0))
    return pl.pallas_call(
        functools.partial(project_kernel, scale=math.sqrt(3.0 / total_coords)),
        out_shape=[out, out],
        grid_spec=pltpu.PrefetchScalarGridSpec(
            num_scalar_prefetch=1,
            grid=(FEATS // FEAT_TILE,),
            in_specs=[pl.BlockSpec((exam_dev, coord_dev), lambda i, s: (0, 0))],
            out_specs=[block, block],
            scratch_shapes=[pltpu.VMEM((coord_dev, 128), jnp.int32)],
        ),
        compiler_params=pltpu.CompilerParams(
            dimension_semantics=("arbitrary",), vmem_limit_bytes=48 * 2**20
        ),
        name="project",
    )(projection_seed, gradients)


def dot_f32(a, b):
    return jnp.dot(a, b, precision=lax.Precision.HIGHEST, preferred_element_type=jnp.float32)


def score_kernel(feat_ref, target_ref, out_ref, picked_ref, sem):
    groups, half, width = feat_ref.shape
    chip = lax.axis_index("z") * lax.axis_size("x") + lax.axis_index("x")
    first = pl.multiple_of(chip * BLOCK, BLOCK)
    copy = pltpu.make_async_copy(
        target_ref.at[:, lax.axis_index("c"), :, pl.ds(first, BLOCK)], picked_ref, sem
    )
    copy.start()
    feats = feat_ref[...].reshape(groups * half, width)
    examples = groups * half
    fisher = lax.dot_general(
        feats, feats, (((0,), (0,)), ((), ())), preferred_element_type=jnp.float32
    ) / examples
    row = lax.broadcasted_iota(jnp.int32, (width, width), 0)
    col = lax.broadcasted_iota(jnp.int32, (width, width), 1)
    identity = (row == col).astype(jnp.float32)
    trace_value = jnp.sum(fisher * identity)
    damped = fisher + (DAMPING * trace_value) * identity
    total = jnp.sum(damped * identity)
    iterate = identity / total
    product = damped / total
    for step in range(STEPS):
        if step < STEPS - 1:
            both = jnp.concatenate([iterate, product], 0)
            both = 2.0 * both - dot_f32(both, product)
            iterate, product = both[:width], both[width:]
        else:
            iterate = 2.0 * iterate - dot_f32(iterate, product)
    inverse_bf = iterate.astype(jnp.bfloat16)
    mine = feat_ref[pl.ds(2 * lax.axis_index("y"), 2)].reshape(2 * half, width)
    conditioned = jnp.dot(mine, inverse_bf, preferred_element_type=jnp.float32).astype(jnp.bfloat16)
    copy.wait()
    picked = picked_ref[...].reshape(-1, width)
    partial = lax.dot_general(
        picked, conditioned, (((1,), (1,)), ((), ())), preferred_element_type=jnp.float32
    )
    out_ref[...] = partial.reshape(out_ref.shape).astype(out_ref.dtype)


def partial_scores(feats, targets):
    chips, cores, rows, _ = targets.shape
    return pl.pallas_call(
        score_kernel,
        out_shape=jax.ShapeDtypeStruct((chips, rows, 2 * feats.shape[1]), jnp.float32),
        in_specs=[pl.BlockSpec(memory_space=pltpu.VMEM), pl.BlockSpec(memory_space=pl.ANY)],
        out_specs=pl.BlockSpec(memory_space=pltpu.VMEM),
        scratch_shapes=[
            pltpu.VMEM((chips, rows, BLOCK), jnp.bfloat16),
            pltpu.SemaphoreType.DMA,
        ],
        name="scores",
    )(feats, targets)


def spread(array, axes):
    return lax.all_to_all(array, axes, split_axis=0, concat_axis=0, tiled=True)


def on_device(gradients, projection_seed, target_features):
    own, send = project(gradients, projection_seed)
    other = lax.ppermute(send, "c", [(0, 1), (1, 0)])
    chip_sum = (own + other).astype(jnp.bfloat16)
    pieces = spread(chip_sum, ("z", "x"))
    feats = jnp.sum(pieces.astype(jnp.float32), 0).astype(jnp.bfloat16)
    groups = lax.axis_size(("y", "c"))
    every = spread(jnp.broadcast_to(feats[None], (groups, *feats.shape)), ("y", "c"))
    chips = lax.axis_size(("z", "x"))
    rows = target_features.shape[0] // (2 * chips)
    partial = partial_scores(every, target_features.reshape(chips, 2, rows, FEATS))
    return jnp.sum(spread(partial, ("z", "x")), 0)


def solution(mesh):
    size = mesh.shape["param"]
    z, x, c, y = 8, 4, 2, mesh.shape["ex"]
    assert z * x * c == size
    inner = Mesh(mesh.devices.reshape(z, x, c, y), ("z", "x", "c", "y"))
    param = ("z", "x", "c")
    return jax.shard_map(
        on_device,
        mesh=inner,
        in_specs=(P("y", param), P(), P()),
        out_specs=P(param, "y"),
        check_vma=False,
    )
```

time: 354 us -> 112 us (0.32)
  waiting for transfers between devices: 183 us -> 2.29 us
  matrix products: 96.2 us -> 0 us
  Pallas kernels: 0 us -> 51.7 us
  blocking collectives: 35.9 us -> 51.2 us
  between operations: 15.6 us -> 0.69 us
  other arithmetic: 9.49 us -> 0.88 us
  local copies, waits for them, and re-layouts: 5.78 us -> 1.6 us
    reduce_scatter x1 -> x0, waiting for transfers between devices: 140 us -> none  [on_device(): lax.psum_scatter(pieces.reshape(feats_owned * lax.axis_size('param'), exa...]
    dot_general x31 -> x0, matrix products: 96.2 us -> none  [the longest x8 79.4 us: project_piece(): return jnp.dot(gradients, matrix, preferred_element_type=jnp.float32).T]
    pallas_call x0 -> x2, Pallas kernels: none -> 51.7 us  [the longest x1 45.5 us: project(): pl.pallas_call(functools.partial(project_kernel, scale=math.sqrt(3.0 / to...]
    psum x1 -> x0, waiting for transfers between devices: 42.4 us -> none  [on_device(): fisher = lax.psum(partial_fisher, 'ex') / examples_total]
    all_to_all x2 -> x3, blocking collectives: 35.9 us -> 51.2 us  [spread(): return lax.all_to_all(array, axes, split_axis=0, concat_axis=0, tiled=True)]
    mul x17 -> x0, other arithmetic: 5.03 us -> none  [the longest x16 5.03 us: hashed(): mixed = row_index * 73856093 ^ col_index * 19349663 ^ seed_value * 83492791]
    dynamic_slice x8 -> x0, local copies, waits for them, and re-layouts: 4.72 us -> none  [on_device(): pieces = lax.map(project_piece, starts)]
  transfers between devices with their start and end apart: 3 -> 1, of which waited for: 3 -> 1; matrix products, arithmetic and copies ran while one was open for 0% -> 0% of each run, Pallas kernels for 0% -> 0%
where the time goes in v1:
time: 112 us
  Pallas kernels  51.7 us (46%)
  blocking collectives  51.2 us (46%)
  starting transfers between devices  3.31 us (3%)
  waiting for transfers between devices  2.29 us (2%)
  local copies, waits for them, and re-layouts  1.6 us (1%)
    all_to_all x3, blocking collectives, spread(): return lax.all_to_all(array, axes, split_axis=0, concat_axis=0, tiled=True)  51.2 us
    pallas_call x1, Pallas kernels, project(): pl.pallas_call(functools.partial(project_kernel, scale=math.sqrt(3.0 / to...  45.5 us
    pallas_call x1, Pallas kernels, partial_scores(): pl.pallas_call(score_kernel, out_shape=jax.ShapeDtypeStruct((chips, rows,...  6.17 us
    ppermute x1, starting transfers between devices, on_device(): other = lax.ppermute(send, 'c', [(0, 1), (1, 0)])  3.31 us
    ppermute x1, waiting for transfers between devices, on_device(): other = lax.ppermute(send, 'c', [(0, 1), (1, 0)])  2.29 us
  transfers between devices with their start and end apart: 1, of which 1 were waited for; matrix products, arithmetic and copies ran while one was open for 0% of the time, Pallas kernels for 0%

profile of v1, /device:TPU:1, one launch (start us, length us, event | category | flops | bytes accessed | tf_op | source)
XLA Modules:
  0.0 111.6 jit_solution(6477281094681261427)
XLA Ops:
  0.7 0.0 copy-start
  0.7 1.6 %copy-done = bf16[128,8192]{1,0:T(8,128)(2,1)S(1)} copy-done((bf16[128,8192]{1,0:T(8,128)(2,1)S(1)}, bf16[128,8192]{1,0:T(8,128)(2,1)}, u32[]{:S(2)}) %copy-start) | copy-done | bytes 2097176
  2.2 45.5 %project.1 = (f32[32,64,128]{2,1,0:T(8,128)S(1)}, f32[32,64,128]{2,1,0:T(8,128)S(1)}) custom-call(s32[1]{0:T(128)S(6)} %copy.4.seed_ref, bf16[128,8192]{1,0:T(8,128)(2,1)S(1)} %copy-done), custom_call_target="tpu_custom_call" | custom-call | tf_op jit(solution)/shard_map/project/pallas_call | solution.py:95
  47.8 3.3 %collective-permute-start = (f32[32,64,128]{2,1,0:T(8,128)S(1)}, f32[32,64,128]{2,1,0:T(8,128)S(1)}, u32[]{:S(2)}, u32[]{:S(2)}) collective-permute-start(f32[32,64,128]{2,1,0:T(8,128)S(1)} %get-tuple-element.8), channel_id=1, source_target_pairs={{0,4},{4,0},{1,5},{5,1},{2,6},{6,2},{3,7},{7,3},{8,12},{12,8},{9,1... | collective-permute-start | bytes 3145736 | tf_op jit(solution)/shard_map/ppermute | solution.py:176
  51.1 2.3 %collective-permute-done = f32[32,64,128]{2,1,0:T(8,128)S(1)} collective-permute-done((f32[32,64,128]{2,1,0:T(8,128)S(1)}, f32[32,64,128]{2,1,0:T(8,128)S(1)}, u32[]{:S(2)}, u32[]{:S(2)}) %collective-permute-start) | collective-permute-done | bytes 1048608 | tf_op jit(solution)/shard_map/ppermute | solution.py:176
  53.4 0.2 add_convert_fusion
  53.5 25.7 %all_to_all.15 = bf16[32,64,128]{2,1,0:T(8,128)(2,1)S(1)} all-to-all(bf16[32,64,128]{2,1,0:T(8,128)(2,1)S(1)} %add_convert_fusion), channel_id=1, replica_groups=mesh['z'=8,'x'=4,'c'=2,'y'=4] {'z','x'}, dimensions={0} | all-to-all | bytes 1048576 | tf_op jit(solution)/shard_map/all_to_all | solution.py:171
  79.3 0.1 reduce_sum.21
  79.4 11.8 %all_to_all.16.feat_ref = bf16[8,64,128]{2,1,0:T(8,128)(2,1)} all-to-all(bf16[8,64,128]{2,1,0:T(8,128)(2,1)S(1)} %broadcast_in_dim.2), channel_id=1, replica_groups=mesh['z'=8,'x'=4,'c'=2,'y'=4] {'y','c'}, dimensions={0} | all-to-all | bytes 262144 | tf_op jit(solution)/shard_map/all_to_all | solution.py:171
  91.2 6.2 %scores.1 = f32[32,8,128]{2,1,0:T(8,128)} custom-call(bf16[8,64,128]{2,1,0:T(8,128)(2,1)} %all_to_all.16.feat_ref, bf16[32,2,8,4096]{3,2,1,0:T(8,128)(2,1)} %bitcast.1), custom_call_target="tpu_custom_call" | custom-call | tf_op jit(solution)/shard_map/scores/pallas_call | solution.py:157
  97.3 13.7 %all_to_all.17 = f32[32,8,128]{2,1,0:T(8,128)S(1)} all-to-all(f32[32,8,128]{2,1,0:T(8,128)} %scores.1), channel_id=1, replica_groups=mesh['z'=8,'x'=4,'c'=2,'y'=4] {'z','x'}, dimensions={0} | all-to-all | bytes 262144 | tf_op jit(solution)/shard_map/all_to_all | solution.py:171
  111.0 0.6 reduce_sum.22
  (1 shorter events, 0.0 us)
Async XLA Ops:
  0.7 1.6 %copy-start = (bf16[128,8192]{1,0:T(8,128)(2,1)S(1)}, bf16[128,8192]{1,0:T(8,128)(2,1)}, u32[]{:S(2)}) copy-start(bf16[128,8192]{1,0:T(8,128)(2,1)} %grad_ref.1) | copy-start | bytes 6291460
  47.8 5.6 %collective-permute-start = (f32[32,64,128]{2,1,0:T(8,128)S(1)}, f32[32,64,128]{2,1,0:T(8,128)S(1)}, u32[]{:S(2)}, u32[]{:S(2)}) collective-permute-start(f32[32,64,128]{2,1,0:T(8,128)S(1)} %get-tuple-element.8), channel_id=1, source_target_pairs={{0,4},{4,0},{1,5},{5,1},{2,6},{6,2},{3,7},{7,3},{8,12},{12,8},{9,1... | collective-permute-start | bytes 3145736 | tf_op jit(solution)/shard_map/ppermute | solution.py:176

commit v2 on v1

--- a/solution.py
+++ b/solution.py
@@ -9,6 +9,9 @@
 from jax.sharding import Mesh
 from jax.sharding import PartitionSpec as P
 
+PARAM = ("z", "xh", "xl", "c")
+CHIPS = ("z", "xh", "xl")
+
 FEATS = 4096
 BLOCK = 128
 STEPS = 10
@@ -30,13 +33,12 @@
     return value ^ jnp.right_shift(value, 13)
 
 
-def project_kernel(seed_ref, grad_ref, own_ref, send_ref, rows_ref, *, scale):
+def project_kernel(seed_ref, grad_ref, own_ref, send_ref, rows_ref, *, scale, first_feat):
     step = pl.program_id(0)
     coord_dev = grad_ref.shape[1]
     half = own_ref.shape[1]
     core = lax.axis_index("c")
-    chip = lax.axis_index("z") * lax.axis_size("x") + lax.axis_index("x")
-    row_start = (chip * lax.axis_size("c") + core) * coord_dev
+    row_start = lax.axis_index(PARAM) * coord_dev
 
     @pl.when(step == 0)
     def _():
@@ -50,7 +52,7 @@
 
     columns = []
     for lane_tile in range(FEAT_TILE // 128):
-        first = step * FEAT_TILE + lane_tile * 128
+        first = first_feat + step * FEAT_TILE + lane_tile * 128
         col = first + lax.broadcasted_iota(jnp.int32, (1, 128), 1)
         columns.append(fold13(col * COL_MUL ^ seed_ref[0] * SEED_MUL) ^ TOP_BIT)
 
@@ -86,18 +88,20 @@
             send_ref[j] = part[:half]
 
 
-def project(gradients, projection_seed):
+def project(gradients, projection_seed, first_feat, feats):
     exam_dev, coord_dev = gradients.shape
-    total_coords = coord_dev * lax.axis_size(("z", "x", "c"))
-    blocks = FEATS // BLOCK
+    total_coords = coord_dev * lax.axis_size(PARAM)
+    blocks = feats // BLOCK
     out = jax.ShapeDtypeStruct((blocks, exam_dev // 2, BLOCK), jnp.float32)
     block = pl.BlockSpec((FEAT_TILE // BLOCK, exam_dev // 2, BLOCK), lambda i, s: (i, 0, 0))
     return pl.pallas_call(
-        functools.partial(project_kernel, scale=math.sqrt(3.0 / total_coords)),
+        functools.partial(
+            project_kernel, scale=math.sqrt(3.0 / total_coords), first_feat=first_feat
+        ),
         out_shape=[out, out],
         grid_spec=pltpu.PrefetchScalarGridSpec(
             num_scalar_prefetch=1,
-            grid=(FEATS // FEAT_TILE,),
+            grid=(feats // FEAT_TILE,),
             in_specs=[pl.BlockSpec((exam_dev, coord_dev), lambda i, s: (0, 0))],
             out_specs=[block, block],
             scratch_shapes=[pltpu.VMEM((coord_dev, 128), jnp.int32)],
@@ -105,6 +109,11 @@
         compiler_params=pltpu.CompilerParams(
             dimension_semantics=("arbitrary",), vmem_limit_bytes=48 * 2**20
         ),
+        cost_estimate=pl.CostEstimate(
+            flops=2 * exam_dev * coord_dev * feats,
+            bytes_accessed=2 * coord_dev * feats,
+            transcendentals=0,
+        ),
         name="project",
     )(projection_seed, gradients)
 
@@ -114,15 +123,15 @@
 
 
 def score_kernel(feat_ref, target_ref, out_ref, picked_ref, sem):
-    groups, half, width = feat_ref.shape
-    chip = lax.axis_index("z") * lax.axis_size("x") + lax.axis_index("x")
-    first = pl.multiple_of(chip * BLOCK, BLOCK)
+    groups, part, width = feat_ref.shape
+    block = lax.axis_index(("xl", "z", "xh"))
+    first = pl.multiple_of(block * BLOCK, BLOCK)
     copy = pltpu.make_async_copy(
         target_ref.at[:, lax.axis_index("c"), :, pl.ds(first, BLOCK)], picked_ref, sem
     )
     copy.start()
-    feats = feat_ref[...].reshape(groups * half, width)
-    examples = groups * half
+    feats = feat_ref[...].reshape(groups * part, width)
+    examples = groups * part
     fisher = lax.dot_general(
         feats, feats, (((0,), (0,)), ((), ())), preferred_element_type=jnp.float32
     ) / examples
@@ -142,7 +151,8 @@
         else:
             iterate = 2.0 * iterate - dot_f32(iterate, product)
     inverse_bf = iterate.astype(jnp.bfloat16)
-    mine = feat_ref[pl.ds(2 * lax.axis_index("y"), 2)].reshape(2 * half, width)
+    base = 4 * lax.axis_index("y")
+    mine = jnp.concatenate([feat_ref[base + i] for i in (0, 2, 1, 3)], 0)
     conditioned = jnp.dot(mine, inverse_bf, preferred_element_type=jnp.float32).astype(jnp.bfloat16)
     copy.wait()
     picked = picked_ref[...].reshape(-1, width)
@@ -153,10 +163,10 @@
 
 
 def partial_scores(feats, targets):
-    chips, cores, rows, _ = targets.shape
+    chips, _, rows, _ = targets.shape
     return pl.pallas_call(
         score_kernel,
-        out_shape=jax.ShapeDtypeStruct((chips, rows, 2 * feats.shape[1]), jnp.float32),
+        out_shape=jax.ShapeDtypeStruct((chips, rows, 4 * feats.shape[1]), jnp.bfloat16),
         in_specs=[pl.BlockSpec(memory_space=pltpu.VMEM), pl.BlockSpec(memory_space=pl.ANY)],
         out_specs=pl.BlockSpec(memory_space=pltpu.VMEM),
         scratch_shapes=[
@@ -171,30 +181,35 @@
     return lax.all_to_all(array, axes, split_axis=0, concat_axis=0, tiled=True)
 
 
-def on_device(gradients, projection_seed, target_features):
-    own, send = project(gradients, projection_seed)
+def reduced(gradients, projection_seed, part):
+    feats = FEATS // 2
+    own, send = project(gradients, projection_seed, part * feats, feats)
     other = lax.ppermute(send, "c", [(0, 1), (1, 0)])
     chip_sum = (own + other).astype(jnp.bfloat16)
-    pieces = spread(chip_sum, ("z", "x"))
-    feats = jnp.sum(pieces.astype(jnp.float32), 0).astype(jnp.bfloat16)
-    groups = lax.axis_size(("y", "c"))
-    every = spread(jnp.broadcast_to(feats[None], (groups, *feats.shape)), ("y", "c"))
-    chips = lax.axis_size(("z", "x"))
+    chips = lax.axis_size(CHIPS)
+    pieces = spread(chip_sum.reshape(chips, -1, BLOCK), CHIPS)
+    return jnp.sum(pieces.astype(jnp.float32), 0).astype(jnp.bfloat16)
+
+
+def on_device(gradients, projection_seed, target_features):
+    both = jnp.stack([reduced(gradients, projection_seed, part) for part in range(2)])
+    _, part, width = both.shape
+    sent = jnp.broadcast_to(both[None, :, None], (lax.axis_size("y"), 2, 2, part, width))
+    every = spread(sent.reshape(-1, part, width), ("y", "xl", "c"))
+    chips = lax.axis_size(CHIPS)
     rows = target_features.shape[0] // (2 * chips)
     partial = partial_scores(every, target_features.reshape(chips, 2, rows, FEATS))
-    return jnp.sum(spread(partial, ("z", "x")), 0)
+    return jnp.sum(spread(partial, CHIPS).astype(jnp.float32), 0)
 
 
 def solution(mesh):
-    size = mesh.shape["param"]
-    z, x, c, y = 8, 4, 2, mesh.shape["ex"]
-    assert z * x * c == size
-    inner = Mesh(mesh.devices.reshape(z, x, c, y), ("z", "x", "c", "y"))
-    param = ("z", "x", "c")
+    z, xh, xl, c, y = 8, 2, 2, 2, mesh.shape["ex"]
+    assert z * xh * xl * c == mesh.shape["param"]
+    inner = Mesh(mesh.devices.reshape(z, xh, xl, c, y), (*PARAM, "y"))
     return jax.shard_map(
         on_device,
         mesh=inner,
-        in_specs=(P("y", param), P(), P()),
-        out_specs=P(param, "y"),
+        in_specs=(P("y", PARAM), P(), P()),
+        out_specs=P(PARAM, "y"),
         check_vma=False,
     )

time: 112 us -> 123 us (1.098)
  blocking collectives: 51.2 us -> 26.9 us
  waiting for transfers between devices: 2.29 us -> 21.2 us
  starting transfers between devices: 3.31 us -> 17.3 us
  other arithmetic: 0.88 us -> 2.26 us
    all_to_all x3 -> x2, blocking collectives: 51.2 us -> 26.9 us  [spread(): return lax.all_to_all(array, axes, split_axis=0, concat_axis=0, tiled=True)]
    all_to_all x0 -> x2, waiting for transfers between devices: none -> 21.2 us  [spread(): return lax.all_to_all(array, axes, split_axis=0, concat_axis=0, tiled=True)]
    all_to_all x0 -> x2, starting transfers between devices: none -> 13.9 us  [spread(): return lax.all_to_all(array, axes, split_axis=0, concat_axis=0, tiled=True)]
    ppermute x1 -> x2, waiting for transfers between devices: 2.29 us -> 0.01 us  [reduced(): other = lax.ppermute(send, 'c', [(0, 1), (1, 0)])]
    convert_element_type x1 -> x2, other arithmetic: 0.16 us -> 1.52 us  [reduced(): chip_sum = (own + other).astype(jnp.bfloat16)]
    pallas_call x1 -> x2, Pallas kernels: 45.5 us -> 46.4 us  [project(): pl.pallas_call(functools.partial(project_kernel, scale=math.sqrt(3.0 / to...]
    ppermute x1 -> x2, starting transfers between devices: 3.31 us -> 3.43 us  [reduced(): other = lax.ppermute(send, 'c', [(0, 1), (1, 0)])]
  transfers between devices with their start and end apart: 1 -> 4, of which waited for: 1 -> 2; matrix products, arithmetic and copies ran while one was open for 0% -> 1% of each run, Pallas kernels for 0% -> 19%
where the time goes in v2:
time: 123 us
  Pallas kernels  52.5 us (43%)
  blocking collectives  26.9 us (22%)
  waiting for transfers between devices  21.2 us (17%)
  starting transfers between devices  17.3 us (14%)
  other arithmetic  2.26 us (2%)
  local copies, waits for them, and re-layouts  1.61 us (1%)
    pallas_call x2, Pallas kernels, project(): pl.pallas_call(functools.partial(project_kernel, scale=math.sqrt(3.0 / to...  46.4 us
    all_to_all x2, blocking collectives, spread(): return lax.all_to_all(array, axes, split_axis=0, concat_axis=0, tiled=True)  26.9 us
    all_to_all x2, waiting for transfers between devices, spread(): return lax.all_to_all(array, axes, split_axis=0, concat_axis=0, tiled=True)  21.2 us
    all_to_all x2, starting transfers between devices, spread(): return lax.all_to_all(array, axes, split_axis=0, concat_axis=0, tiled=True)  13.9 us
    pallas_call x1, Pallas kernels, partial_scores(): pl.pallas_call(score_kernel, out_shape=jax.ShapeDtypeStruct((chips, rows,...  6.15 us
    ppermute x2, starting transfers between devices, reduced(): other = lax.ppermute(send, 'c', [(0, 1), (1, 0)])  3.43 us
  transfers between devices with their start and end apart: 4, of which 2 were waited for; matrix products, arithmetic and copies ran while one was open for 1% of the time, Pallas kernels for 19%

profile of v2, /device:TPU:1, one launch (start us, length us, event | category | flops | bytes accessed | tf_op | source)
XLA Modules:
  0.0 122.5 jit_solution(757883346011811199)
XLA Ops:
  0.7 0.0 copy-start
  0.7 1.6 %copy-done = bf16[128,8192]{1,0:T(8,128)(2,1)S(1)} copy-done((bf16[128,8192]{1,0:T(8,128)(2,1)S(1)}, bf16[128,8192]{1,0:T(8,128)(2,1)}, u32[]{:S(2)}) %copy-start) | copy-done | bytes 2097176
  2.2 23.2 %project.3 = (f32[16,64,128]{2,1,0:T(8,128)S(1)}, f32[16,64,128]{2,1,0:T(8,128)S(1)}) custom-call(s32[1]{0:T(128)S(6)} %copy.4.seed_ref, bf16[128,8192]{1,0:T(8,128)(2,1)S(1)} %copy-done), custom_call_target="tpu_custom_call" | custom-call | flops 4294967296 | bytes 33554432 | tf_op jit(solution)/shard_map/project/pallas_call | solution.py:97
  25.4 3.3 %collective-permute-start.1 = (f32[16,64,128]{2,1,0:T(8,128)S(1)}, f32[16,64,128]{2,1,0:T(8,128)S(1)}, u32[]{:S(2)}, u32[]{:S(2)}) collective-permute-start(f32[16,64,128]{2,1,0:T(8,128)S(1)} %get-tuple-element.12), channel_id=1, source_target_pairs={{0,4},{4,0},{1,5},{5,1},{2,6},{6,2},{3,7},{7,3},{8,12},{12,8},{9,1... | collective-permute-start | bytes 1572872 | tf_op jit(solution)/shard_map/ppermute | solution.py:187
  28.7 23.2 %project.2 = (f32[16,64,128]{2,1,0:T(8,128)S(1)}, f32[16,64,128]{2,1,0:T(8,128)S(1)}) custom-call(s32[1]{0:T(128)S(6)} %copy.4.seed_ref, bf16[128,8192]{1,0:T(8,128)(2,1)S(1)} %copy-done), custom_call_target="tpu_custom_call" | custom-call | flops 4294967296 | bytes 33554432 | tf_op jit(solution)/shard_map/project/pallas_call | solution.py:97
  51.9 0.1 collective-permute-start
  52.1 0.0 collective-permute-done.1
  52.1 0.8 add_convert_fusion
  52.8 9.3 %all-to-all-start.1 = ((bf16[32,32,128]{2,1,0:T(8,128)(2,1)}), bf16[32,32,128]{2,1,0:T(8,128)(2,1)S(1)}, u32[]{:S(2)}, u32[]{:S(2)}) async-start(bf16[32,32,128]{2,1,0:T(8,128)(2,1)} %bitcast.2), calls=%async_computation.1 | async-start | bytes 524288 | tf_op jit(solution)/shard_map/all_to_all | solution.py:181
  62.2 0.0 collective-permute-done
  62.2 0.8 add_convert_fusion.1
  62.9 10.8 %all-to-all-done.1 = bf16[32,32,128]{2,1,0:T(8,128)(2,1)S(1)} async-done(((bf16[32,32,128]{2,1,0:T(8,128)(2,1)}), bf16[32,32,128]{2,1,0:T(8,128)(2,1)S(1)}, u32[]{:S(2)}, u32[]{:S(2)}) %all-to-all-start.1) | async-done | bytes 262176 | tf_op jit(solution)/shard_map/all_to_all | solution.py:181
  73.8 4.5 %all-to-all-start = ((bf16[32,32,128]{2,1,0:T(8,128)(2,1)}), bf16[32,32,128]{2,1,0:T(8,128)(2,1)S(1)}, u32[]{:S(2)}, u32[]{:S(2)}) async-start(bf16[32,32,128]{2,1,0:T(8,128)(2,1)} %bitcast), calls=%async_computation | async-start | bytes 524288 | tf_op jit(solution)/shard_map/all_to_all | solution.py:181
  78.3 0.1 reduce_sum.34
  78.4 10.4 %all-to-all-done = bf16[32,32,128]{2,1,0:T(8,128)(2,1)S(1)} async-done(((bf16[32,32,128]{2,1,0:T(8,128)(2,1)}), bf16[32,32,128]{2,1,0:T(8,128)(2,1)S(1)}, u32[]{:S(2)}, u32[]{:S(2)}) %all-to-all-start) | async-done | bytes 262176 | tf_op jit(solution)/shard_map/all_to_all | solution.py:181
  88.8 0.1 reduce_sum.33
  88.9 14.0 %all_to_all.20.feat_ref = bf16[16,32,128]{2,1,0:T(8,128)(2,1)} all-to-all(bf16[16,32,128]{2,1,0:T(8,128)(2,1)S(1)} %bitcast.7), channel_id=1, replica_groups=mesh['z'=8,'xh'=2,'xl'=2,'c'=2,'y'=4] {'y','xl','c'}, dimensions={0} | all-to-all | bytes 262144 | tf_op jit(solution)/shard_map/all_to_all | solution.py:181
  102.8 6.2 %scores.1 = bf16[32,8,128]{2,1,0:T(8,128)(2,1)} custom-call(bf16[16,32,128]{2,1,0:T(8,128)(2,1)} %all_to_all.20.feat_ref, bf16[32,2,8,4096]{3,2,1,0:T(8,128)(2,1)} %bitcast.6), custom_call_target="tpu_custom_call" | custom-call | tf_op jit(solution)/shard_map/scores/pallas_call | solution.py:167
  109.0 12.9 %all_to_all.21 = bf16[32,8,128]{2,1,0:T(8,128)(2,1)S(1)} all-to-all(bf16[32,8,128]{2,1,0:T(8,128)(2,1)} %scores.1), channel_id=1, replica_groups=mesh['z'=8,'xh'=2,'xl'=2,'c'=2,'y'=4] {'z','xh','xl'}, dimensions={0} | all-to-all | bytes 131072 | tf_op jit(solution)/shard_map/all_to_all | solution.py:181
  121.9 0.6 convert_reduce_fusion
  (2 shorter events, 0.0 us)
Async XLA Ops:
  0.7 1.6 %copy-start = (bf16[128,8192]{1,0:T(8,128)(2,1)S(1)}, bf16[128,8192]{1,0:T(8,128)(2,1)}, u32[]{:S(2)}) copy-start(bf16[128,8192]{1,0:T(8,128)(2,1)} %grad_ref.3) | copy-start | bytes 6291460
  25.4 26.6 %collective-permute-start.1 = (f32[16,64,128]{2,1,0:T(8,128)S(1)}, f32[16,64,128]{2,1,0:T(8,128)S(1)}, u32[]{:S(2)}, u32[]{:S(2)}) collective-permute-start(f32[16,64,128]{2,1,0:T(8,128)S(1)} %get-tuple-element.12), channel_id=1, source_target_pairs={{0,4},{4,0},{1,5},{5,1},{2,6},{6,2},{3,7},{7,3},{8,12},{12,8},{9,1... | collective-permute-start | bytes 1572872 | tf_op jit(solution)/shard_map/ppermute | solution.py:187
  51.9 10.2 %collective-permute-start = (f32[16,64,128]{2,1,0:T(8,128)S(1)}, f32[16,64,128]{2,1,0:T(8,128)S(1)}, u32[]{:S(2)}, u32[]{:S(2)}) collective-permute-start(f32[16,64,128]{2,1,0:T(8,128)S(1)} %get-tuple-element.10), channel_id=1, source_target_pairs={{0,4},{4,0},{1,5},{5,1},{2,6},{6,2},{3,7},{7,3},{8,12},{12,8},{9,1... | collective-permute-start | bytes 1572872 | tf_op jit(solution)/shard_map/ppermute | solution.py:187
  52.8 20.9 %all-to-all-start.1 = ((bf16[32,32,128]{2,1,0:T(8,128)(2,1)}), bf16[32,32,128]{2,1,0:T(8,128)(2,1)S(1)}, u32[]{:S(2)}, u32[]{:S(2)}) async-start(bf16[32,32,128]{2,1,0:T(8,128)(2,1)} %bitcast.2), calls=%async_computation.1 | async-start | bytes 524288 | tf_op jit(solution)/shard_map/all_to_all | solution.py:181
  73.8 15.0 %all-to-all-start = ((bf16[32,32,128]{2,1,0:T(8,128)(2,1)}), bf16[32,32,128]{2,1,0:T(8,128)(2,1)S(1)}, u32[]{:S(2)}, u32[]{:S(2)}) async-start(bf16[32,32,128]{2,1,0:T(8,128)(2,1)} %bitcast), calls=%async_computation | async-start | bytes 524288 | tf_op jit(solution)/shard_map/all_to_all | solution.py:181
